TPU v7x, 32 devices: a whole 2x2x4 slice. The times are simulated.
32 devices in a mesh: dom: 8 (over z, y), ka: 4 (over x, core).
Axes of the slice: x: 2, y: 2, z: 4, core: 2. Of those that a mesh axis runs over, the one named last changes fastest.
Arguments:
- x_blocks: bfloat16 [64, 64, 2048], P('dom', None, 'ka'), may hold values from -0.29882812 to 0.29882812
- col_index: int32 [64, 32], P('dom'), may hold values from 0 to 63, as said below
- prod_index: int32 [64, 32], P('dom'), may hold values from 0 to 63, as said below
Outputs:
- purified: bfloat16 [64, 64, 2048], P('dom', None, 'ka')
Inputs may be any that keep to these rules, and one draw needn't show every extreme that they name: `col_index`: row i lists 32 distinct block columns (i + o) mod 64 with offsets o between -16 and 16, in ascending order of o; the offsets 0, -16 and 16 are always among them. `prod_index`: row i lists 32 distinct block columns (i + o) mod 64 with offsets o between -16 and 16, in ascending order of o; the offsets 0, -16 and 16 are always among them.
All inputs are finite; a program needn't handle non-finite values.
Results may differ from a plain program's by a relative error of at most 0.013.
Values may be sent and summed in bfloat16 or wider, within the bound.
No kernel may reach another device: no remote copies, remote signals or barrier semaphores. Data moves between devices by JAX's collectives and lax.ppermute only.
A program may use at most 128 MiB of HBM per device.

v0:
```python
import jax
import jax.numpy as jnp
from jax import lax
from jax.sharding import PartitionSpec as P


def passed_along(value, axis, steps):
    count = lax.axis_size(axis)
    pairs = [(source, (source + steps) % count) for source in range(count)]
    return lax.ppermute(value, axis, pairs)


def block_table(padded_rows, ext_offsets, left_places, left_offsets, target_offsets):
    empty_slot = ext_offsets.shape[1]
    relative = target_offsets[None, :] - left_offsets[:, None]
    row_offsets = jnp.take(ext_offsets, left_places, axis=0)
    matches = row_offsets[:, None, :] == relative[:, :, None]
    present = jnp.any(matches, axis=2)
    slot_index = jnp.where(present, jnp.argmax(matches, axis=2), empty_slot)
    return padded_rows[left_places[:, None], :, slot_index, :]


def per_device(x_blocks, col_index, prod_index):
    row_count = x_blocks.shape[0]
    block_size = x_blocks.shape[1]
    stored_slots = col_index.shape[1]
    slot_groups = lax.axis_size("ka")
    group_index = lax.axis_index("ka")
    left_slots = x_blocks.shape[2] // block_size
    prod_slots = prod_index.shape[1]
    prod_group = prod_slots // slot_groups
    total_rows = row_count * lax.axis_size("dom")
    reach_rows = 2 * row_count
    local_rows = lax.axis_index("dom") * row_count + jnp.arange(row_count, dtype=jnp.int32)
    col_offsets = (col_index - local_rows[:, None] + reach_rows) % total_rows - reach_rows
    prod_offsets = (prod_index - local_rows[:, None] + reach_rows) % total_rows - reach_rows
    offset_send = col_offsets.astype(jnp.bfloat16)
    received = {}
    full_rows = lax.all_gather(x_blocks, "ka", axis=2, tiled=True)
    for distance in (2, 1, -1, -2):
        received[distance] = passed_along((full_rows, offset_send), "dom", distance)
    extended = jnp.concatenate(
        [received[2][0], received[1][0], full_rows, received[-1][0], received[-2][0]], axis=0
    )
    ext_offsets = jnp.concatenate(
        [received[2][1], received[1][1], offset_send, received[-1][1], received[-2][1]], axis=0
    ).astype(jnp.int32)
    extended_rows = extended.reshape(5 * row_count, block_size, stored_slots, block_size)
    zero_slot = jnp.zeros((5 * row_count, block_size, 1, block_size), extended_rows.dtype)
    padded_rows = jnp.concatenate([extended_rows, zero_slot], axis=2)
    row_numbers = jnp.arange(row_count, dtype=jnp.int32)

    def first_row(row_index):
        own_offsets = lax.dynamic_slice_in_dim(
            col_offsets[row_index], group_index * left_slots, left_slots
        )
        places = reach_rows + row_index + own_offsets
        gathered = block_table(
            padded_rows, ext_offsets, places, own_offsets, prod_offsets[row_index]
        )
        left_blocks = x_blocks[row_index].reshape(block_size, left_slots, block_size)
        square = jnp.einsum(
            "asb,stbc->atc", left_blocks, gathered, preferred_element_type=jnp.float32
        )
        return square.reshape(block_size, prod_slots * block_size)

    square_all = lax.psum(lax.map(first_row, row_numbers).astype(jnp.bfloat16), "ka").astype(
        jnp.float32
    )
    square_low = square_all.astype(jnp.bfloat16)
    square_own = lax.dynamic_slice_in_dim(
        square_all, group_index * prod_group * block_size, prod_group * block_size, 2
    )

    def second_whole(row_index):
        all_offsets = prod_offsets[row_index]
        targets = lax.dynamic_slice_in_dim(all_offsets, group_index * prod_group, prod_group)
        places = reach_rows + row_index + all_offsets
        gathered = block_table(padded_rows, ext_offsets, places, all_offsets, targets)
        gathered = gathered.reshape(slot_groups, prod_group, prod_group, block_size, block_size)
        left_blocks = square_low[row_index].reshape(block_size, slot_groups, prod_group, block_size)
        pieces = jnp.einsum(
            "agsb,gstbc->gatc", left_blocks, gathered, preferred_element_type=jnp.float32
        )
        rounded = lax.optimization_barrier(pieces.astype(jnp.bfloat16))
        return jnp.sum(rounded.astype(jnp.float32), axis=0).reshape(
            block_size, prod_group * block_size
        )

    cube_own = lax.map(second_whole, row_numbers)
    return (3.0 * square_own - 2.0 * cube_own).astype(jnp.bfloat16)


def solution(mesh):
    return jax.shard_map(
        per_device,
        mesh=mesh,
        in_specs=(P("dom", None, "ka"), P("dom", None), P("dom", None)),
        out_specs=P("dom", None, "ka"),
        check_vma=False,
    )
```

profile of v0, /device:TPU:0, one launch (start us, length us, event | category | flops | bytes accessed | tf_op | source)
XLA Modules:
  0.0 743.3 jit_solution(16485561505347758447)
XLA Ops:
  7.3 26.9 %all-gather.2.cloned.1.call-done = bf16[8,64,2048]{2,1,0:T(8,128)(2,1)} async-done(((bf16[8,64,512]{2,1,0:T(8,128)(2,1)}), bf16[8,64,2048]{2,1,0:T(8,128)(2,1)}) %all-gather.2.cloned.1.call-update) | async-done | bytes 2097168 | tf_op jit(solution)/shard_map/all_gather | solution.py:39
  43.3 130.7 %collective-permute-done = bf16[8,32]{1,0:T(8,128)(2,1)S(1)} collective-permute-done((bf16[8,32]{1,0:T(8,128)(2,1)S(1)}, bf16[8,32]{1,0:T(8,128)(2,1)S(1)}, u32[]{:S(2)}, u32[]{:S(2)}) %collective-permute-start) | collective-permute-done | bytes 544 | tf_op jit(solution)/shard_map/ppermute | solution.py:10
  200.2 30.4 %reshape.233 = bf16[40,64,32,64]{3,2,1,0:T(8,128)(2,1)} reshape(bf16[40,64,2048]{2,1,0:T(8,128)(2,1)} %constant_dynamic-update-slice_fusion.6) | data formatting | bytes 20971520 | tf_op jit(solution)/shard_map/reshape | solution.py:48
  230.5 14.9 %copy.50 = bf16[40,64,32,64]{3,1,2,0:T(8,128)(2,1)S(1)} copy(bf16[40,64,32,64]{3,2,1,0:T(8,128)(2,1)} %reshape.233) | data formatting | bytes 20971520
  245.4 10.4 %concatenate.25.clone = bf16[40,64,33,64]{3,1,2,0:T(8,128)(2,1)} pad(bf16[40,64,32,64]{3,1,2,0:T(8,128)(2,1)S(1)} %copy.50, bf16[]{:T(256)} %constant.286.clone.1), padding=0_0x0_0x0_1x0_0 | pad | bytes 21299202 | tf_op jit(solution)/shard_map/concatenate | solution.py:50
  255.8 247.0 %while.26 = (s32[]{:T(128)}, bf16[8,64,2048]{2,1,0:T(8,128)(2,1)}, s32[8]{0:T(128)S(1)}, bf16[8,64,512]{2,1,0:T(8,128)(2,1)}, s32[8,32]{1,0:T(8,128)S(1)}, /*ind...) while((s32[]{:T(128)}, bf16[8,64,2048]{2,1,0:T(8,128)(2,1)}, ...), condition=%wide.region_3.4_spmd, body=%wide.region_0.3_spmd.sunk | while | flops 134301040 | bytes 15554775 | solution.py:67
  261.2 10.6 %gather_fusion.1 = bf16[256,64,64]{2,1,0:T(8,128)(2,1)} fusion(bf16[40,64,33,64]{3,1,2,0:T(8,128)(2,1)} %get-tuple-element.580, s32[256]{0:T(256)S(1)} %reshape.290), kind=kCustom, calls=%fused_computation.1.clone.1 | custom fusion | bytes 4196352 | tf_op jit(solution)/shard_map/while/body/eval_jaxpr/gather | solution.py:20
  271.8 6.9 copy.71
  292.1 10.6 %gather_fusion.1 = bf16[256,64,64]{2,1,0:T(8,128)(2,1)} fusion(bf16[40,64,33,64]{3,1,2,0:T(8,128)(2,1)} %get-tuple-element.580, s32[256]{0:T(256)S(1)} %reshape.290), kind=kCustom, calls=%fused_computation.1.clone.1 | custom fusion | bytes 4196352 | tf_op jit(solution)/shard_map/while/body/eval_jaxpr/gather | solution.py:20
  302.6 6.9 copy.71
  322.9 10.6 %gather_fusion.1 = bf16[256,64,64]{2,1,0:T(8,128)(2,1)} fusion(bf16[40,64,33,64]{3,1,2,0:T(8,128)(2,1)} %get-tuple-element.580, s32[256]{0:T(256)S(1)} %reshape.290), kind=kCustom, calls=%fused_computation.1.clone.1 | custom fusion | bytes 4196352 | tf_op jit(solution)/shard_map/while/body/eval_jaxpr/gather | solution.py:20
  333.5 6.9 copy.71
  353.8 10.6 %gather_fusion.1 = bf16[256,64,64]{2,1,0:T(8,128)(2,1)} fusion(bf16[40,64,33,64]{3,1,2,0:T(8,128)(2,1)} %get-tuple-element.580, s32[256]{0:T(256)S(1)} %reshape.290), kind=kCustom, calls=%fused_computation.1.clone.1 | custom fusion | bytes 4196352 | tf_op jit(solution)/shard_map/while/body/eval_jaxpr/gather | solution.py:20
  364.4 6.9 copy.71
  384.7 10.6 %gather_fusion.1 = bf16[256,64,64]{2,1,0:T(8,128)(2,1)} fusion(bf16[40,64,33,64]{3,1,2,0:T(8,128)(2,1)} %get-tuple-element.580, s32[256]{0:T(256)S(1)} %reshape.290), kind=kCustom, calls=%fused_computation.1.clone.1 | custom fusion | bytes 4196352 | tf_op jit(solution)/shard_map/while/body/eval_jaxpr/gather | solution.py:20
  395.3 6.9 copy.71
  415.6 10.6 %gather_fusion.1 = bf16[256,64,64]{2,1,0:T(8,128)(2,1)} fusion(bf16[40,64,33,64]{3,1,2,0:T(8,128)(2,1)} %get-tuple-element.580, s32[256]{0:T(256)S(1)} %reshape.290), kind=kCustom, calls=%fused_computation.1.clone.1 | custom fusion | bytes 4196352 | tf_op jit(solution)/shard_map/while/body/eval_jaxpr/gather | solution.py:20
  426.1 6.9 copy.71
  446.4 10.6 %gather_fusion.1 = bf16[256,64,64]{2,1,0:T(8,128)(2,1)} fusion(bf16[40,64,33,64]{3,1,2,0:T(8,128)(2,1)} %get-tuple-element.580, s32[256]{0:T(256)S(1)} %reshape.290), kind=kCustom, calls=%fused_computation.1.clone.1 | custom fusion | bytes 4196352 | tf_op jit(solution)/shard_map/while/body/eval_jaxpr/gather | solution.py:20
  457.0 6.9 copy.71
  477.3 10.6 %gather_fusion.1 = bf16[256,64,64]{2,1,0:T(8,128)(2,1)} fusion(bf16[40,64,33,64]{3,1,2,0:T(8,128)(2,1)} %get-tuple-element.580, s32[256]{0:T(256)S(1)} %reshape.290), kind=kCustom, calls=%fused_computation.1.clone.1 | custom fusion | bytes 4196352 | tf_op jit(solution)/shard_map/while/body/eval_jaxpr/gather | solution.py:20
  487.9 6.9 copy.71
  502.8 51.8 %all-reduce.3.cloned.1.call-done = bf16[8,64,2048]{2,1,0:T(8,128)(2,1)} async-done(((bf16[8,64,2048]{2,1,0:T(8,128)(2,1)}), bf16[8,64,2048]{2,1,0:T(8,128)(2,1)}) %all-reduce.3.cloned.1.call-update) | async-done | bytes 2097168 | tf_op jit(solution)/shard_map/psum | solution.py:67
  554.6 179.8 %while.27 = (s32[]{:T(128)}, f32[8,64,512]{2,1,0:T(8,128)S(1)}, s32[8]{0:T(128)S(1)}, bf16[8,64,2048]{2,1,0:T(8,128)(2,1)}, s32[8,32]{1,0:T(8,128)S(1)}, /*index...) while((s32[]{:T(128)}, f32[8,64,512]{2,1,0:T(8,128)S(1)}, ...), condition=%wide.region_9.10_spmd, body=%wide.region_5.9_spmd.sunk | while | flops 134662560 | bytes 9091591 | solution.py:90
  561.4 10.6 %gather_fusion.3 = bf16[256,64,64]{2,1,0:T(8,128)(2,1)} fusion(bf16[40,64,33,64]{3,1,2,0:T(8,128)(2,1)} %get-tuple-element.619, s32[256]{0:T(256)S(1)} %reshape.295), kind=kCustom, calls=%fused_computation.3.clone.1 | custom fusion | bytes 4196352 | tf_op jit(solution)/shard_map/while/body/eval_jaxpr/gather | solution.py:20
  583.9 10.6 %gather_fusion.3 = bf16[256,64,64]{2,1,0:T(8,128)(2,1)} fusion(bf16[40,64,33,64]{3,1,2,0:T(8,128)(2,1)} %get-tuple-element.619, s32[256]{0:T(256)S(1)} %reshape.295), kind=kCustom, calls=%fused_computation.3.clone.1 | custom fusion | bytes 4196352 | tf_op jit(solution)/shard_map/while/body/eval_jaxpr/gather | solution.py:20
  606.4 10.6 %gather_fusion.3 = bf16[256,64,64]{2,1,0:T(8,128)(2,1)} fusion(bf16[40,64,33,64]{3,1,2,0:T(8,128)(2,1)} %get-tuple-element.619, s32[256]{0:T(256)S(1)} %reshape.295), kind=kCustom, calls=%fused_computation.3.clone.1 | custom fusion | bytes 4196352 | tf_op jit(solution)/shard_map/while/body/eval_jaxpr/gather | solution.py:20
  628.9 10.6 %gather_fusion.3 = bf16[256,64,64]{2,1,0:T(8,128)(2,1)} fusion(bf16[40,64,33,64]{3,1,2,0:T(8,128)(2,1)} %get-tuple-element.619, s32[256]{0:T(256)S(1)} %reshape.295), kind=kCustom, calls=%fused_computation.3.clone.1 | custom fusion | bytes 4196352 | tf_op jit(solution)/shard_map/while/body/eval_jaxpr/gather | solution.py:20
  651.3 10.6 %gather_fusion.3 = bf16[256,64,64]{2,1,0:T(8,128)(2,1)} fusion(bf16[40,64,33,64]{3,1,2,0:T(8,128)(2,1)} %get-tuple-element.619, s32[256]{0:T(256)S(1)} %reshape.295), kind=kCustom, calls=%fused_computation.3.clone.1 | custom fusion | bytes 4196352 | tf_op jit(solution)/shard_map/while/body/eval_jaxpr/gather | solution.py:20
  673.8 10.6 %gather_fusion.3 = bf16[256,64,64]{2,1,0:T(8,128)(2,1)} fusion(bf16[40,64,33,64]{3,1,2,0:T(8,128)(2,1)} %get-tuple-element.619, s32[256]{0:T(256)S(1)} %reshape.295), kind=kCustom, calls=%fused_computation.3.clone.1 | custom fusion | bytes 4196352 | tf_op jit(solution)/shard_map/while/body/eval_jaxpr/gather | solution.py:20
  696.3 10.6 %gather_fusion.3 = bf16[256,64,64]{2,1,0:T(8,128)(2,1)} fusion(bf16[40,64,33,64]{3,1,2,0:T(8,128)(2,1)} %get-tuple-element.619, s32[256]{0:T(256)S(1)} %reshape.295), kind=kCustom, calls=%fused_computation.3.clone.1 | custom fusion | bytes 4196352 | tf_op jit(solution)/shard_map/while/body/eval_jaxpr/gather | solution.py:20
  718.8 10.6 %gather_fusion.3 = bf16[256,64,64]{2,1,0:T(8,128)(2,1)} fusion(bf16[40,64,33,64]{3,1,2,0:T(8,128)(2,1)} %get-tuple-element.619, s32[256]{0:T(256)S(1)} %reshape.295), kind=kCustom, calls=%fused_computation.3.clone.1 | custom fusion | bytes 4196352 | tf_op jit(solution)/shard_map/while/body/eval_jaxpr/gather | solution.py:20
  (351 shorter events, 198.0 us)
Async XLA Ops:
  6.5 27.7 %all-gather.2.cloned.1.call-start = ((), (), s32[]{:S(2)}) async-start(), calls=%async_computation | async-start | bytes 2621440 | tf_op jit(solution)/shard_map/all_gather | solution.py:39
  7.3 547.3 %all-reduce.3.cloned.1.call-start = ((), (), s32[]{:S(2)}) async-start(), calls=%async_computation.1 | async-start | bytes 4194304 | tf_op jit(solution)/shard_map/psum | solution.py:67
  34.2 153.3 %collective-permute-start.4 = (bf16[8,64,2048]{2,1,0:T(8,128)(2,1)}, bf16[8,64,2048]{2,1,0:T(8,128)(2,1)}, u32[]{:S(2)}, u32[]{:S(2)}) collective-permute-start(bf16[8,64,2048]{2,1,0:T(8,128)(2,1)} %all-gather.2.cloned.1.call-done), channel_id=1, source_target_pairs={{0,8},{4,12},{8,16},{12,20},{16,24},{20,28},{24,0},{28,4},{1,9},{5... | collective-permute-start | bytes 6291464 | tf_op jit(solution)/shard_map/ppermute | solution.py:10
  35.7 155.1 %collective-permute-start.5 = (bf16[8,64,2048]{2,1,0:T(8,128)(2,1)}, bf16[8,64,2048]{2,1,0:T(8,128)(2,1)}, u32[]{:S(2)}, u32[]{:S(2)}) collective-permute-start(bf16[8,64,2048]{2,1,0:T(8,128)(2,1)} %all-gather.2.cloned.1.call-done), channel_id=1, source_target_pairs={{0,4},{4,8},{8,12},{12,16},{16,20},{20,24},{24,28},{28,0},{1,5},{5... | collective-permute-start | bytes 6291464 | tf_op jit(solution)/shard_map/ppermute | solution.py:10
  37.2 158.4 %collective-permute-start.6 = (bf16[8,64,2048]{2,1,0:T(8,128)(2,1)}, bf16[8,64,2048]{2,1,0:T(8,128)(2,1)}, u32[]{:S(2)}, u32[]{:S(2)}) collective-permute-start(bf16[8,64,2048]{2,1,0:T(8,128)(2,1)} %all-gather.2.cloned.1.call-done), channel_id=1, source_target_pairs={{0,28},{4,0},{8,4},{12,8},{16,12},{20,16},{24,20},{28,24},{1,29},{... | collective-permute-start | bytes 6291464 | tf_op jit(solution)/shard_map/ppermute | solution.py:10
  40.4 158.2 %collective-permute-start.7 = (bf16[8,64,2048]{2,1,0:T(8,128)(2,1)}, bf16[8,64,2048]{2,1,0:T(8,128)(2,1)S(1)}, u32[]{:S(2)}, u32[]{:S(2)}) collective-permute-start(bf16[8,64,2048]{2,1,0:T(8,128)(2,1)} %all-gather.2.cloned.1.call-done), channel_id=1, source_target_pairs={{0,24},{4,28},{8,0},{12,4},{16,8},{20,12},{24,16},{28,20},{1,25},{... | collective-permute-start | bytes 6291464 | tf_op jit(solution)/shard_map/ppermute | solution.py:10
  41.7 132.2 %collective-permute-start = (bf16[8,32]{1,0:T(8,128)(2,1)S(1)}, bf16[8,32]{1,0:T(8,128)(2,1)S(1)}, u32[]{:S(2)}, u32[]{:S(2)}) collective-permute-start(bf16[8,32]{1,0:T(8,128)(2,1)S(1)} %get-tuple-element.415), channel_id=1, source_target_pairs={{0,8},{4,12},{8,16},{12,20},{16,24},{20,28},{24,0},{28,4},{1,9},{5... | collective-permute-start | bytes 1544 | tf_op jit(solution)/shard_map/ppermute | solution.py:10
  174.0 6.3 collective-permute-start.1
  180.3 3.6 collective-permute-start.2
  183.9 3.6 collective-permute-start.3
  187.5 6.5 copy-start
Sparse Core Ops, SparseCore 0:
  8.9 25.2 all-gather.1
  502.9 51.6 all-reduce.2
where the time goes:
time: 748 us; the launch traced here: 743 us
  local copies, waits for them, and re-layouts  382 us (51%)
  waiting for transfers between devices  222 us (30%)
  loops' own time  42.4 us (6%)
  other arithmetic  38.2 us (5%)
  matrix products  35 us (5%)
  between operations  13.5 us (2%)
  starting transfers between devices  9.75 us (1%)
    gather x16, local copies, waits for them, and re-layouts, block_table(): return padded_rows[left_places[:, None], :, slot_index, :]  169 us
    ppermute x8, waiting for transfers between devices, passed_along(): return lax.ppermute(value, axis, pairs)  143 us
    dot_general x16, local copies, waits for them, and re-layouts, first_row(): jnp.einsum('asb,stbc->atc', left_blocks, gathered, preferred_element_type...  101 us
    psum x1, waiting for transfers between devices, per_device(): lax.psum(lax.map(first_row, row_numbers).astype(jnp.bfloat16), 'ka')  51.8 us
    reshape x1, local copies, waits for them, and re-layouts, per_device(): extended.reshape(5 * row_count, block_size, stored_slots, block_size)  30.4 us
    all_gather x1, waiting for transfers between devices, per_device(): full_rows = lax.all_gather(x_blocks, 'ka', axis=2, tiled=True)  26.9 us
    unnamed x11, local copies, waits for them, and re-layouts  26.1 us
    dot_general x8, matrix products, second_whole(): jnp.einsum('agsb,gstbc->gatc', left_blocks, gathered, preferred_element_t...  25.1 us
  transfers between devices with their start and end apart: 10, of which 6 were waited for; matrix products, arithmetic and copies ran while one was open for 2% of the time, Pallas kernels for 0%

commit v1 on v0

v1 whole, which is shorter than its diff:
```python
import functools

import jax
import jax.numpy as jnp
from jax import lax
from jax.experimental import pallas as pl
from jax.experimental.pallas import tpu as pltpu
from jax.sharding import PartitionSpec as P

CHUNKS = 1
WINDOWS = 5
PIECES = 3


def permuted(value, pairs):
    return lax.ppermute(value, ("dom", "ka"), pairs)


def routes(dom_count, ka_count):
    def pairs(target):
        out = []
        for dom in range(dom_count):
            for group in range(ka_count):
                to = target(dom, group, group // 2, dom % 2)
                if to is not None:
                    out.append((dom * ka_count + group, (to[0] % dom_count) * ka_count + to[1]))
        return out

    return {
        "za": pairs(lambda d, g, x, y: (d + 2 if x else d - 2, g)),
        "zb": pairs(lambda d, g, x, y: (d - 2 if x else d + 2, g)),
        "x": pairs(lambda d, g, x, y: (d, g ^ 2)),
        "y": pairs(lambda d, g, x, y: (d ^ 1, g)),
        "y_same": pairs(lambda d, g, x, y: (d ^ 1, g) if x == y else None),
        "y_other": pairs(lambda d, g, x, y: (d ^ 1, g) if x != y else None),
        "d_same": pairs(lambda d, g, x, y: (d ^ 1, g ^ 2) if x == y else None),
        "d_other": pairs(lambda d, g, x, y: (d ^ 1, g ^ 2) if x != y else None),
        "core": pairs(lambda d, g, x, y: (d, g ^ 1)),
        "core_za": pairs(lambda d, g, x, y: (d, g ^ 1) if g in (0, 3) else None),
        "core_zb": pairs(lambda d, g, x, y: (d, g ^ 1) if g in (1, 2) else None),
    }


def shifted(wide, first, count):
    return wide[:, first:first + count]


def spread(pieces, shift, width, threshold):
    wide = jnp.concatenate(pieces, axis=1)
    low = shifted(wide, shift * 64, width * 64)
    high = shifted(wide, (shift - 1) * 64, width * 64)
    place = lax.broadcasted_iota(jnp.int32, low.shape, 1)
    zero = jnp.zeros_like(low)
    return jnp.where(place < threshold * 64, low, jnp.where(place >= threshold * 64 + 64, high, zero))


def kept(total, row, threshold, width):
    low = shifted(total, row * 64, width)
    high = shifted(total, (row + 1) * 64, width)
    place = lax.broadcasted_iota(jnp.int32, low.shape, 1)
    return jnp.where(place < threshold * 64, low, high)


def fill_left(left_ref, rows_of, thresholds, row_count):
    for row in range(row_count):
        blocks = rows_of(row)
        pad = jnp.zeros((64, 512), blocks[0].dtype)
        left_ref[row * 64:(row + 1) * 64, :] = spread(
            [pad] + blocks + [pad], 8 - row, WINDOWS * 8, thresholds(row)
        )


def product(left_ref, table_ref, total_ref):
    def step(tile, carry):
        cols = pl.ds(pl.multiple_of(tile * 256, 256), 256)
        total_ref[:, cols] = jnp.dot(left_ref[...], table_ref[:, cols], preferred_element_type=jnp.float32)
        return carry

    lax.fori_loop(0, table_ref.shape[1] // 256, step, 0)


def square_kernel(item_count, chunk_rows, meta_ref, *refs):
    items = refs[:item_count]
    table_ref, square_ref, low_ref = refs[item_count:item_count + 3]
    store, left_store, left_ref, total_ref, sems, left_sems = refs[item_count + 3:]
    row_count = square_ref.shape[0]
    base = 0
    dest_at = 65
    left_at = 65 + item_count
    valid_at = 65 + 2 * item_count

    def copies(number):
        rows = pl.ds((number % CHUNKS) * chunk_rows, chunk_rows)
        dest = meta_ref[dest_at + number]
        left = meta_ref[left_at + number]
        main = pltpu.make_async_copy(items[number], store.at[jnp.maximum(dest, 0), rows], sems.at[number])
        side = pltpu.make_async_copy(items[number], left_store.at[jnp.maximum(left, 0), rows], left_sems.at[number])
        return dest, left, main, side

    for number in range(item_count):
        dest, left, main, side = copies(number)
        pl.when(dest >= 0)(main.start)
        pl.when(left >= 0)(side.start)
    for place in range(WINDOWS * PIECES):
        @pl.when(meta_ref[valid_at + place] == 0)
        def _():
            store[place] = jnp.zeros(store.shape[1:], store.dtype)
    for number in range(item_count):
        dest, left, main, side = copies(number)
        pl.when(dest >= 0)(main.wait)
        pl.when(left >= 0)(side.wait)

    fill_left(left_ref, lambda row: [left_store[h, row] for h in range(4)], lambda row: meta_ref[40 + row], row_count)

    def window(delta, carry):
        for row in range(row_count):
            blocks = [store[delta * PIECES + piece, row] for piece in range(PIECES)]
            at = pl.ds(pl.multiple_of(delta * 512 + row * 64, 64), 64)
            table_ref[at, :] = spread(blocks, 8 - row, 16, meta_ref[base + delta * 8 + row])
        return carry

    lax.fori_loop(0, WINDOWS, window, 0)
    product(left_ref, table_ref, total_ref)
    for row in range(row_count):
        picked = kept(total_ref[row * 64:(row + 1) * 64, :], row, meta_ref[48 + row], 512)
        square_ref[row] = picked
        low_ref[row] = picked.astype(low_ref.dtype)


def cube_kernel(meta_ref, own_ref, core_ref, x_ref, far_ref, table_ref, square_ref, out_ref, store, left_ref, total_ref):
    row_count = out_ref.shape[0]
    group = meta_ref[64]
    for bits, ref in enumerate((own_ref, core_ref, x_ref, far_ref)):
        store[group ^ bits] = ref[...]
    fill_left(left_ref, lambda row: [store[h, row] for h in range(4)], lambda row: meta_ref[56 + row], row_count)
    product(left_ref, table_ref, total_ref)
    for row in range(row_count):
        cube = kept(total_ref[row * 64:(row + 1) * 64, :], row, meta_ref[48 + row], 512)
        out_ref[row] = (3.0 * square_ref[row] - 2.0 * cube).astype(out_ref.dtype)


def missing_places(index, rows, total_rows, reach):
    places = (index - rows[:, None] + reach) % total_rows
    slots = jnp.arange(index.shape[1], dtype=jnp.int32)[None, :]
    return jnp.sum((places == slots).astype(jnp.int32), axis=1)


def per_device(dom_count, ka_count, x_blocks, col_index, prod_index):
    row_count, block, width = x_blocks.shape
    reach = 2 * row_count
    total_rows = row_count * dom_count
    dom = lax.axis_index("dom")
    group = lax.axis_index("ka")
    x_side, y_side = group // 2, dom % 2
    route = routes(dom_count, ka_count)
    steps = jnp.arange(row_count, dtype=jnp.int32)
    rows = dom * row_count + steps
    col_missing = missing_places(col_index, rows, total_rows, reach)
    prod_missing = missing_places(prod_index, rows, total_rows, reach)

    def along(value, distance):
        return lax.ppermute(value, "dom", [(d, (d - distance) % dom_count) for d in range(dom_count)])

    missing = [col_missing if delta == 0 else along(col_missing, delta) for delta in range(-2, 3)]

    sign = 2 * x_side - 1
    same = x_side == y_side
    chunk_rows = row_count // CHUNKS
    kinds = {}

    def add(name, chunk, array, delta, held, valid):
        kinds.setdefault(name, []).append((array, delta, held, valid))

    for chunk in range(CHUNKS):
        own = x_blocks[chunk * chunk_rows:(chunk + 1) * chunk_rows]
        za = permuted(own, route["za"])
        zb = permuted(own, route["zb"])
        ox = permuted(own, route["x"])
        oy = permuted(own, route["y"])
        do = permuted(own, route["d_other"])
        bx = permuted(za, route["x"])
        by_a = permuted(za, route["y_same"])
        by_b = permuted(zb, route["y_other"])
        da = permuted(za, route["d_same"])
        near = 1 - 2 * y_side
        far = -near
        held = (
            ("own", own, 0, group, True, "core"),
            ("za", za, -2 * sign, group, True, "core_za"),
            ("zb", zb, 2 * sign, group, True, "core_zb"),
            ("ox", ox, 0, group ^ 2, True, "core"),
            ("oy", oy, near, group, True, "core"),
            ("do", do, sign, group ^ 2, jnp.logical_not(same), "core"),
            ("bx", bx, 2 * sign, group ^ 2, True, "core"),
            ("by_a", by_a, far, group, jnp.logical_not(same), "core"),
            ("by_b", by_b, far, group, same, "core"),
            ("da", da, sign, group ^ 2, same, "core"),
        )
        for name, array, delta, shard, valid, core_route in held:
            add(name, chunk, array, delta, shard, valid)
            valid_core = valid
            if core_route == "core_za":
                valid_core = (group == 1) | (group == 2)
            if core_route == "core_zb":
                valid_core = (group == 0) | (group == 3)
            add(name + "_core", chunk, permuted(array, route[core_route]), delta, shard ^ 1, valid_core)

    items, dests, lefts = [], [], []
    for entries in kinds.values():
        for array, delta, shard, valid in entries:
            piece = shard - group + delta + 1
            dest = (delta + 2) * PIECES + piece
            dests.append(jnp.where(valid & (piece >= 0) & (piece < PIECES), dest, -1))
            lefts.append(jnp.where(valid & (jnp.asarray(delta) == 0), shard, -1))
            items.append(array)
    valid_places = []
    for delta in range(-2, 3):
        for piece in range(PIECES):
            shard = group - delta - 1 + piece
            valid_places.append(((shard >= 0) & (shard < ka_count)).astype(jnp.int32))
    table_places = [
        missing[delta + 2] - 8 * (group - delta) + steps for delta in range(-2, 3)
    ]
    meta = jnp.concatenate(
        table_places
        + [col_missing + steps, prod_missing - 8 * group, prod_missing + steps, group[None]]
        + [jnp.stack(dests), jnp.stack(lefts), jnp.stack(valid_places)]
    ).astype(jnp.int32)

    smem = pl.BlockSpec(memory_space=pltpu.SMEM)
    vmem = pl.BlockSpec(memory_space=pltpu.VMEM)
    anywhere = pl.BlockSpec(memory_space=pl.ANY)
    depth = WINDOWS * 8 * block
    table, square, low = pl.pallas_call(
        functools.partial(square_kernel, len(items), chunk_rows),
        out_shape=(
            jax.ShapeDtypeStruct((depth, 16 * block), jnp.bfloat16),
            jax.ShapeDtypeStruct((row_count, block, width), jnp.float32),
            jax.ShapeDtypeStruct((row_count, block, width), jnp.bfloat16),
        ),
        in_specs=[smem] + [anywhere] * len(items),
        out_specs=(vmem, vmem, vmem),
        scratch_shapes=[
            pltpu.VMEM((WINDOWS * PIECES, row_count, block, width), jnp.bfloat16),
            pltpu.VMEM((ka_count, row_count, block, width), jnp.bfloat16),
            pltpu.VMEM((row_count * block, depth), jnp.bfloat16),
            pltpu.VMEM((row_count * block, 16 * block), jnp.float32),
            pltpu.SemaphoreType.DMA((len(items),)),
            pltpu.SemaphoreType.DMA((len(items),)),
        ],
    )(meta, *items)
    low_core = permuted(low, route["core"])
    low_x = permuted(low, route["x"])
    low_far = permuted(low_x, route["core"])
    return pl.pallas_call(
        cube_kernel,
        out_shape=jax.ShapeDtypeStruct((row_count, block, width), jnp.bfloat16),
        in_specs=[smem] + [vmem] * 6,
        out_specs=vmem,
        scratch_shapes=[
            pltpu.VMEM((ka_count, row_count, block, width), jnp.bfloat16),
            pltpu.VMEM((row_count * block, depth), jnp.bfloat16),
            pltpu.VMEM((row_count * block, 16 * block), jnp.float32),
        ],
    )(meta, low, low_core, low_x, low_far, table, square)


def solution(mesh):
    return jax.shard_map(
        functools.partial(per_device, mesh.shape["dom"], mesh.shape["ka"]),
        mesh=mesh,
        in_specs=(P("dom", None, "ka"), P("dom", None), P("dom", None)),
        out_specs=P("dom", None, "ka"),
        check_vma=False,
    )
```

time: 748 us -> 125 us (0.17)
  local copies, waits for them, and re-layouts: 382 us -> 2.37 us
  waiting for transfers between devices: 222 us -> 57.9 us
  loops' own time: 42.4 us -> 0 us
  other arithmetic: 38.2 us -> 0.95 us
  matrix products: 35 us -> 0 us
  starting transfers between devices: 9.75 us -> 41.2 us
  Pallas kernels: 0 us -> 22.1 us
  between operations: 13.5 us -> 0.19 us
    gather x32 -> x0, local copies, waits for them, and re-layouts: 178 us -> none  [the longest x16 169 us: block_table(): return padded_rows[left_places[:, None], :, slot_index, :]]
    dot_general x16 -> x0, local copies, waits for them, and re-layouts: 101 us -> none  [first_row(): jnp.einsum('asb,stbc->atc', left_blocks, gathered, preferred_element_type...]
    ppermute x8 -> x26, waiting for transfers between devices: 143 us -> 57.9 us  [the longest x4 31.1 us: along(): lax.ppermute(value, 'dom', [(d, (d - distance) % dom_count) for d in rang...]
    psum x1 -> x0, waiting for transfers between devices: 51.8 us -> none  [per_device(): lax.psum(lax.map(first_row, row_numbers).astype(jnp.bfloat16), 'ka')]
    another operation x2 -> x0, loops' own time: 42.4 us -> none  [the longest x1 21.4 us: per_device(): cube_own = lax.map(second_whole, row_numbers)]
    dot_general x16 -> x0, matrix products: 35 us -> none  [the longest x8 25.1 us: second_whole(): jnp.einsum('agsb,gstbc->gatc', left_blocks, gathered, preferred_element_t...]
    ppermute x8 -> x26, starting transfers between devices: 9.71 us -> 41.2 us  [the longest x22 35.8 us: permuted(): return lax.ppermute(value, ('dom', 'ka'), pairs)]
    reshape x1 -> x0, local copies, waits for them, and re-layouts: 30.4 us -> none  [per_device(): extended.reshape(5 * row_count, block_size, stored_slots, block_size)]
  transfers between devices with their start and end apart: 10 -> 26, of which waited for: 6 -> 11; matrix products, arithmetic and copies ran while one was open for 2% -> 1% of each run, Pallas kernels for 0% -> 0%
where the time goes in v1:
time: 125 us
  waiting for transfers between devices  57.9 us (46%)
  starting transfers between devices  41.2 us (33%)
  Pallas kernels  22.1 us (18%)
  local copies, waits for them, and re-layouts  2.37 us (2%)
    ppermute x22, starting transfers between devices, permuted(): return lax.ppermute(value, ('dom', 'ka'), pairs)  35.8 us
    ppermute x4, waiting for transfers between devices, along(): lax.ppermute(value, 'dom', [(d, (d - distance) % dom_count) for d in rang...  31.1 us
    ppermute x22, waiting for transfers between devices, permuted(): return lax.ppermute(value, ('dom', 'ka'), pairs)  26.8 us
    pallas_call x1, Pallas kernels, per_device(): pl.pallas_call(functools.partial(square_kernel, len(items), chunk_rows),...  13.2 us
    pallas_call x1, Pallas kernels, per_device(): pl.pallas_call(cube_kernel, out_shape=jax.ShapeDtypeStruct((row_count, bl...  8.92 us
    ppermute x4, starting transfers between devices, along(): lax.ppermute(value, 'dom', [(d, (d - distance) % dom_count) for d in rang...  5.39 us
  transfers between devices with their start and end apart: 26, of which 11 were waited for; matrix products, arithmetic and copies ran while one was open for 1% of the time, Pallas kernels for 0%

profile of v1, /device:TPU:0, one launch (start us, length us, event | category | flops | bytes accessed | tf_op | source)
XLA Modules:
  0.0 124.8 jit_solution(6993549827367213071)
XLA Ops:
  0.0 3.0 %collective-permute-start.11 = (bf16[8,64,512]{2,1,0:T(8,128)(2,1)}, bf16[8,64,512]{2,1,0:T(8,128)(2,1)S(1)}, u32[]{:S(2)}, u32[]{:S(2)}) collective-permute-start(bf16[8,64,512]{2,1,0:T(8,128)(2,1)} %refs_0_.1), channel_id=1, source_target_pairs={{0,4},{1,5},{2,6},{3,7},{4,0},{5,1},{6,2},{7,3},{8,12},{9,13},{10,... | collective-permute-start | bytes 1572872 | tf_op jit(solution)/shard_map/ppermute | solution.py:16
  3.0 1.5 %collective-permute-start.9 = (bf16[8,64,512]{2,1,0:T(8,128)(2,1)}, bf16[8,64,512]{2,1,0:T(8,128)(2,1)S(1)}, u32[]{:S(2)}, u32[]{:S(2)}) collective-permute-start(bf16[8,64,512]{2,1,0:T(8,128)(2,1)} %refs_0_.1), channel_id=1, source_target_pairs={{0,2},{1,3},{2,0},{3,1},{4,6},{5,7},{6,4},{7,5},{8,10},{9,11},{10,... | collective-permute-start | bytes 1572872 | tf_op jit(solution)/shard_map/ppermute | solution.py:16
  4.5 1.6 %collective-permute-start.7 = (bf16[8,64,512]{2,1,0:T(8,128)(2,1)}, bf16[8,64,512]{2,1,0:T(8,128)(2,1)S(1)}, u32[]{:S(2)}, u32[]{:S(2)}) collective-permute-start(bf16[8,64,512]{2,1,0:T(8,128)(2,1)} %refs_0_.1), channel_id=1, source_target_pairs={{0,8},{1,9},{2,26},{3,27},{4,12},{5,13},{6,30},{7,31},{8,16},{9,17... | collective-permute-start | bytes 1572872 | tf_op jit(solution)/shard_map/ppermute | solution.py:16
  6.1 2.2 %collective-permute-start.5 = (bf16[8,64,512]{2,1,0:T(8,128)(2,1)}, bf16[8,64,512]{2,1,0:T(8,128)(2,1)S(1)}, u32[]{:S(2)}, u32[]{:S(2)}) collective-permute-start(bf16[8,64,512]{2,1,0:T(8,128)(2,1)} %refs_0_.1), channel_id=1, source_target_pairs={{0,24},{1,25},{2,10},{3,11},{4,28},{5,29},{6,14},{7,15},{8,0},{9,1... | collective-permute-start | bytes 1572872 | tf_op jit(solution)/shard_map/ppermute | solution.py:16
  8.3 0.9 convert_reduce_fusion
  9.2 1.9 %collective-permute-start.3 = (s32[8]{0:T(128)S(1)}, s32[8]{0:T(128)S(1)}, u32[]{:S(2)}, u32[]{:S(2)}) collective-permute-start(s32[8]{0:T(128)S(1)} %get-tuple-element.12), channel_id=1, source_target_pairs={{0,24},{4,28},{8,0},{12,4},{16,8},{20,12},{24,16},{28,20},{1,25},{... | collective-permute-start | bytes 104 | tf_op jit(solution)/shard_map/ppermute | solution.py:162
  11.1 19.3 %collective-permute-done.3 = s32[8]{0:T(128)S(1)} collective-permute-done((s32[8]{0:T(128)S(1)}, s32[8]{0:T(128)S(1)}, u32[]{:S(2)}, u32[]{:S(2)}) %collective-permute-start.3) | collective-permute-done | bytes 64 | tf_op jit(solution)/shard_map/ppermute | solution.py:162
  30.4 2.1 %collective-permute-start.2 = (s32[8]{0:T(128)S(1)}, s32[8]{0:T(128)S(1)}, u32[]{:S(2)}, u32[]{:S(2)}) collective-permute-start(s32[8]{0:T(128)S(1)} %get-tuple-element.12), channel_id=1, source_target_pairs={{0,28},{4,0},{8,4},{12,8},{16,12},{20,16},{24,20},{28,24},{1,29},{... | collective-permute-start | bytes 104 | tf_op jit(solution)/shard_map/ppermute | solution.py:162
  32.6 1.4 %collective-permute-done.2 = s32[8]{0:T(128)S(1)} collective-permute-done((s32[8]{0:T(128)S(1)}, s32[8]{0:T(128)S(1)}, u32[]{:S(2)}, u32[]{:S(2)}) %collective-permute-start.2) | collective-permute-done | bytes 64 | tf_op jit(solution)/shard_map/ppermute | solution.py:162
  34.0 1.4 %collective-permute-start.1 = (s32[8]{0:T(128)S(1)}, s32[8]{0:T(128)S(1)}, u32[]{:S(2)}, u32[]{:S(2)}) collective-permute-start(s32[8]{0:T(128)S(1)} %get-tuple-element.12), channel_id=1, source_target_pairs={{0,4},{4,8},{8,12},{12,16},{16,20},{20,24},{24,28},{28,0},{1,5},{5... | collective-permute-start | bytes 104 | tf_op jit(solution)/shard_map/ppermute | solution.py:162
  35.4 5.0 %collective-permute-done.1 = s32[8]{0:T(128)S(1)} collective-permute-done((s32[8]{0:T(128)S(1)}, s32[8]{0:T(128)S(1)}, u32[]{:S(2)}, u32[]{:S(2)}) %collective-permute-start.1) | collective-permute-done | bytes 64 | tf_op jit(solution)/shard_map/ppermute | solution.py:162
  40.4 5.4 %collective-permute-done = s32[8]{0:T(128)S(1)} collective-permute-done((s32[8]{0:T(128)S(1)}, s32[8]{0:T(128)S(1)}, u32[]{:S(2)}, u32[]{:S(2)}) %collective-permute-start) | collective-permute-done | bytes 64 | tf_op jit(solution)/shard_map/ppermute | solution.py:162
  45.7 0.7 collective-permute-start.13
  46.5 0.6 collective-permute-start.12
  47.1 1.3 %collective-permute-start.19 = (bf16[8,64,512]{2,1,0:T(8,128)(2,1)S(1)}, bf16[8,64,512]{2,1,0:T(8,128)(2,1)S(1)}, u32[]{:S(2)}, u32[]{:S(2)}) collective-permute-start(bf16[8,64,512]{2,1,0:T(8,128)(2,1)S(1)} %collective-permute-done.7.refs_4_), channel_id=1, source_target_pairs={{2,6},{3,7},{4,0},{5,1},{10,14},{11,15},{12,8},{13,9},{18,22},{19,... | collective-permute-start | bytes 1572872 | tf_op jit(solution)/shard_map/ppermute | solution.py:16
  48.4 1.3 %collective-permute-start.8 = (bf16[8,64,512]{2,1,0:T(8,128)(2,1)S(1)}, bf16[8,64,512]{2,1,0:T(8,128)(2,1)}, u32[]{:S(2)}, u32[]{:S(2)}) collective-permute-start(bf16[8,64,512]{2,1,0:T(8,128)(2,1)S(1)} %collective-permute-done.7.refs_4_), channel_id=1, source_target_pairs={{1,0},{2,3},{5,4},{6,7},{9,8},{10,11},{13,12},{14,15},{17,16},{18,... | collective-permute-start | bytes 1572872 | tf_op jit(solution)/shard_map/ppermute | solution.py:16
  49.8 4.4 %collective-permute-start.21 = (bf16[8,64,512]{2,1,0:T(8,128)(2,1)S(1)}, bf16[8,64,512]{2,1,0:T(8,128)(2,1)}, u32[]{:S(2)}, u32[]{:S(2)}) collective-permute-start(bf16[8,64,512]{2,1,0:T(8,128)(2,1)S(1)} %collective-permute-done.5.refs_2_), channel_id=1, source_target_pairs={{0,6},{1,7},{6,0},{7,1},{8,14},{9,15},{14,8},{15,9},{16,22},{17,23... | collective-permute-start | bytes 1572872 | tf_op jit(solution)/shard_map/ppermute | solution.py:16
  54.2 14.4 %collective-permute-start.17 = (bf16[8,64,512]{2,1,0:T(8,128)(2,1)S(1)}, bf16[8,64,512]{2,1,0:T(8,128)(2,1)}, u32[]{:S(2)}, u32[]{:S(2)}) collective-permute-start(bf16[8,64,512]{2,1,0:T(8,128)(2,1)S(1)} %collective-permute-done.5.refs_2_), channel_id=1, source_target_pairs={{0,4},{1,5},{6,2},{7,3},{8,12},{9,13},{14,10},{15,11},{16,20},{17,... | collective-permute-start | bytes 1572872 | tf_op jit(solution)/shard_map/ppermute | solution.py:16
  68.5 8.4 %collective-permute-done.19.refs_16_ = bf16[8,64,512]{2,1,0:T(8,128)(2,1)S(1)} collective-permute-done((bf16[8,64,512]{2,1,0:T(8,128)(2,1)S(1)}, bf16[8,64,512]{2,1,0:T(8,128)(2,1)S(1)}, u32[]{:S(2)}, u32[]{:S(2)}) %collective-permute-start.19) | collective-permute-done | bytes 524320 | tf_op jit(solution)/shard_map/ppermute | solution.py:16
  77.0 0.8 copy-done.11
  77.8 2.4 %collective-permute-start.6 = (bf16[8,64,512]{2,1,0:T(8,128)(2,1)S(1)}, bf16[8,64,512]{2,1,0:T(8,128)(2,1)}, u32[]{:S(2)}, u32[]{:S(2)}) collective-permute-start(bf16[8,64,512]{2,1,0:T(8,128)(2,1)S(1)} %collective-permute-done.5.refs_2_), channel_id=1, source_target_pairs={{0,1},{3,2},{4,5},{7,6},{8,9},{11,10},{12,13},{15,14},{16,17},{19,... | collective-permute-start | bytes 1572872 | tf_op jit(solution)/shard_map/ppermute | solution.py:16
  80.9 1.2 collective-permute-done.15.refs_12_
  82.6 0.7 concatenate.3.meta_ref
  83.3 0.5 collective-permute-done.22.refs_19_
  83.8 0.7 collective-permute-done.18.refs_15_
  84.6 0.7 collective-permute-done.16.refs_13_
  85.4 13.2 %shard_map.37 = (bf16[2560,1024]{1,0:T(8,128)(2,1)}, f32[8,64,512]{2,1,0:T(8,128)}, bf16[8,64,512]{2,1,0:T(8,128)(2,1)}) custom-call(s32[120]{0:T(128)} %concatenate.3.meta_ref, bf16[8,64,512]{2,1,0:T(8,128)(2,1)} %refs_0_.1, bf16[8,64,512]{2,1,0:T(8,128)(2,1)} %copy-done.7, bf16[8,64,512]{2,1,0:T(8,128)(2,1)} %copy-done.6, ...), custom_call_target="tpu_custom_call" | custom-call | tf_op jit(solution)/shard_map/pallas_call | solution.py:234
  98.6 1.3 %collective-permute-start.24 = (bf16[8,64,512]{2,1,0:T(8,128)(2,1)}, bf16[8,64,512]{2,1,0:T(8,128)(2,1)S(1)}, u32[]{:S(2)}, u32[]{:S(2)}) collective-permute-start(bf16[8,64,512]{2,1,0:T(8,128)(2,1)} %get-tuple-element.8.own_ref), channel_id=1, source_target_pairs={{0,2},{1,3},{2,0},{3,1},{4,6},{5,7},{6,4},{7,5},{8,10},{9,11},{10,... | collective-permute-start | bytes 1572872 | tf_op jit(solution)/shard_map/ppermute | solution.py:16
  99.9 13.3 %collective-permute-done.24.x_ref = bf16[8,64,512]{2,1,0:T(8,128)(2,1)S(1)} collective-permute-done((bf16[8,64,512]{2,1,0:T(8,128)(2,1)}, bf16[8,64,512]{2,1,0:T(8,128)(2,1)S(1)}, u32[]{:S(2)}, u32[]{:S(2)}) %collective-permute-start.24) | collective-permute-done | bytes 524320 | tf_op jit(solution)/shard_map/ppermute | solution.py:16
  113.1 1.9 %collective-permute-done.25.far_ref = bf16[8,64,512]{2,1,0:T(8,128)(2,1)S(1)} collective-permute-done((bf16[8,64,512]{2,1,0:T(8,128)(2,1)S(1)}, bf16[8,64,512]{2,1,0:T(8,128)(2,1)S(1)}, u32[]{:S(2)}, u32[]{:S(2)}) %collective-permute-start.25) | collective-permute-done | bytes 524320 | tf_op jit(solution)/shard_map/ppermute | solution.py:16
  115.0 0.8 copy-done.2
  115.9 8.9 %shard_map.38 = bf16[8,64,512]{2,1,0:T(8,128)(2,1)} custom-call(s32[120]{0:T(128)} %concatenate.3.meta_ref, bf16[8,64,512]{2,1,0:T(8,128)(2,1)} %get-tuple-element.8.own_ref, bf16[8,64,512]{2,1,0:T(8,128)(2,1)} %copy-done.1, bf16[8,64,512]{2,1,0:T(8,128)(2,1)} %copy-done, bf16[8,64,512]{2,1,0:T(8,128)(2,1)} %copy-done.2, ...), custom_call_target="tpu_custom_call" | custom-call | tf_op jit(solution)/shard_map/pallas_call | solution.py:255
  (54 shorter events, 1.4 us)
Async XLA Ops:
  0.0 45.7 %collective-permute-start.11 = (bf16[8,64,512]{2,1,0:T(8,128)(2,1)}, bf16[8,64,512]{2,1,0:T(8,128)(2,1)S(1)}, u32[]{:S(2)}, u32[]{:S(2)}) collective-permute-start(bf16[8,64,512]{2,1,0:T(8,128)(2,1)} %refs_0_.1), channel_id=1, source_target_pairs={{0,4},{1,5},{2,6},{3,7},{4,0},{5,1},{6,2},{7,3},{8,12},{9,13},{10,... | collective-permute-start | bytes 1572872 | tf_op jit(solution)/shard_map/ppermute | solution.py:16
  3.0 43.5 %collective-permute-start.9 = (bf16[8,64,512]{2,1,0:T(8,128)(2,1)}, bf16[8,64,512]{2,1,0:T(8,128)(2,1)S(1)}, u32[]{:S(2)}, u32[]{:S(2)}) collective-permute-start(bf16[8,64,512]{2,1,0:T(8,128)(2,1)} %refs_0_.1), channel_id=1, source_target_pairs={{0,2},{1,3},{2,0},{3,1},{4,6},{5,7},{6,4},{7,5},{8,10},{9,11},{10,... | collective-permute-start | bytes 1572872 | tf_op jit(solution)/shard_map/ppermute | solution.py:16
  4.5 42.5 %collective-permute-start.7 = (bf16[8,64,512]{2,1,0:T(8,128)(2,1)}, bf16[8,64,512]{2,1,0:T(8,128)(2,1)S(1)}, u32[]{:S(2)}, u32[]{:S(2)}) collective-permute-start(bf16[8,64,512]{2,1,0:T(8,128)(2,1)} %refs_0_.1), channel_id=1, source_target_pairs={{0,8},{1,9},{2,26},{3,27},{4,12},{5,13},{6,30},{7,31},{8,16},{9,17... | collective-permute-start | bytes 1572872 | tf_op jit(solution)/shard_map/ppermute | solution.py:16
  6.1 41.1 %collective-permute-start.5 = (bf16[8,64,512]{2,1,0:T(8,128)(2,1)}, bf16[8,64,512]{2,1,0:T(8,128)(2,1)S(1)}, u32[]{:S(2)}, u32[]{:S(2)}) collective-permute-start(bf16[8,64,512]{2,1,0:T(8,128)(2,1)} %refs_0_.1), channel_id=1, source_target_pairs={{0,24},{1,25},{2,10},{3,11},{4,28},{5,29},{6,14},{7,15},{8,0},{9,1... | collective-permute-start | bytes 1572872 | tf_op jit(solution)/shard_map/ppermute | solution.py:16
  9.2 21.2 %collective-permute-start.3 = (s32[8]{0:T(128)S(1)}, s32[8]{0:T(128)S(1)}, u32[]{:S(2)}, u32[]{:S(2)}) collective-permute-start(s32[8]{0:T(128)S(1)} %get-tuple-element.12), channel_id=1, source_target_pairs={{0,24},{4,28},{8,0},{12,4},{16,8},{20,12},{24,16},{28,20},{1,25},{... | collective-permute-start | bytes 104 | tf_op jit(solution)/shard_map/ppermute | solution.py:162
  30.4 3.6 %collective-permute-start.2 = (s32[8]{0:T(128)S(1)}, s32[8]{0:T(128)S(1)}, u32[]{:S(2)}, u32[]{:S(2)}) collective-permute-start(s32[8]{0:T(128)S(1)} %get-tuple-element.12), channel_id=1, source_target_pairs={{0,28},{4,0},{8,4},{12,8},{16,12},{20,16},{24,20},{28,24},{1,29},{... | collective-permute-start | bytes 104 | tf_op jit(solution)/shard_map/ppermute | solution.py:162
  34.0 6.4 %collective-permute-start.1 = (s32[8]{0:T(128)S(1)}, s32[8]{0:T(128)S(1)}, u32[]{:S(2)}, u32[]{:S(2)}) collective-permute-start(s32[8]{0:T(128)S(1)} %get-tuple-element.12), channel_id=1, source_target_pairs={{0,4},{4,8},{8,12},{12,16},{16,20},{20,24},{24,28},{28,0},{1,5},{5... | collective-permute-start | bytes 104 | tf_op jit(solution)/shard_map/ppermute | solution.py:162
  40.4 5.4 %collective-permute-start = (s32[8]{0:T(128)S(1)}, s32[8]{0:T(128)S(1)}, u32[]{:S(2)}, u32[]{:S(2)}) collective-permute-start(s32[8]{0:T(128)S(1)} %get-tuple-element.12), channel_id=1, source_target_pairs={{0,8},{4,12},{8,16},{12,20},{16,24},{20,28},{24,0},{28,4},{1,9},{5... | collective-permute-start | bytes 104 | tf_op jit(solution)/shard_map/ppermute | solution.py:162
  45.7 2.7 %collective-permute-start.4 = (bf16[8,64,512]{2,1,0:T(8,128)(2,1)}, bf16[8,64,512]{2,1,0:T(8,128)(2,1)S(1)}, u32[]{:S(2)}, u32[]{:S(2)}) collective-permute-start(bf16[8,64,512]{2,1,0:T(8,128)(2,1)} %refs_0_.1), channel_id=1, source_target_pairs={{0,1},{1,0},{2,3},{3,2},{4,5},{5,4},{6,7},{7,6},{8,9},{9,8},{10,11... | collective-permute-start | bytes 1572872 | tf_op jit(solution)/shard_map/ppermute | solution.py:16
  45.7 39.6 %copy-start.3 = (bf16[8,64,512]{2,1,0:T(8,128)(2,1)}, bf16[8,64,512]{2,1,0:T(8,128)(2,1)S(1)}, u32[]{:S(2)}) copy-start(bf16[8,64,512]{2,1,0:T(8,128)(2,1)S(1)} %collective-permute-done.11.refs_8_) | copy-start | bytes 1572868
  45.7 4.0 %collective-permute-start.13 = (bf16[8,64,512]{2,1,0:T(8,128)(2,1)}, bf16[8,64,512]{2,1,0:T(8,128)(2,1)S(1)}, u32[]{:S(2)}, u32[]{:S(2)}) collective-permute-start(bf16[8,64,512]{2,1,0:T(8,128)(2,1)} %refs_0_.1), channel_id=1, source_target_pairs={{2,4},{3,5},{4,2},{5,3},{10,12},{11,13},{12,10},{13,11},{18,20},{1... | collective-permute-start | bytes 1572872 | tf_op jit(solution)/shard_map/ppermute | solution.py:16
  46.5 38.9 %copy-start.4 = (bf16[8,64,512]{2,1,0:T(8,128)(2,1)}, bf16[8,64,512]{2,1,0:T(8,128)(2,1)S(1)}, u32[]{:S(2)}) copy-start(bf16[8,64,512]{2,1,0:T(8,128)(2,1)S(1)} %collective-permute-done.9.refs_6_) | copy-start | bytes 1572868
  46.5 7.7 %collective-permute-start.12 = (bf16[8,64,512]{2,1,0:T(8,128)(2,1)S(1)}, bf16[8,64,512]{2,1,0:T(8,128)(2,1)S(1)}, u32[]{:S(2)}, u32[]{:S(2)}) collective-permute-start(bf16[8,64,512]{2,1,0:T(8,128)(2,1)S(1)} %collective-permute-done.11.refs_8_), channel_id=1, source_target_pairs={{0,1},{1,0},{2,3},{3,2},{4,5},{5,4},{6,7},{7,6},{8,9},{9,8},{10,11... | collective-permute-start | bytes 1572872 | tf_op jit(solution)/shard_map/ppermute | solution.py:16
  47.0 38.3 %copy-start.5 = (bf16[8,64,512]{2,1,0:T(8,128)(2,1)}, bf16[8,64,512]{2,1,0:T(8,128)(2,1)S(1)}, u32[]{:S(2)}) copy-start(bf16[8,64,512]{2,1,0:T(8,128)(2,1)S(1)} %collective-permute-done.7.refs_4_) | copy-start | bytes 1572868
  47.0 21.5 %collective-permute-start.10 = (bf16[8,64,512]{2,1,0:T(8,128)(2,1)S(1)}, bf16[8,64,512]{2,1,0:T(8,128)(2,1)S(1)}, u32[]{:S(2)}, u32[]{:S(2)}) collective-permute-start(bf16[8,64,512]{2,1,0:T(8,128)(2,1)S(1)} %collective-permute-done.9.refs_6_), channel_id=1, source_target_pairs={{0,1},{1,0},{2,3},{3,2},{4,5},{5,4},{6,7},{7,6},{8,9},{9,8},{10,11... | collective-permute-start | bytes 1572872 | tf_op jit(solution)/shard_map/ppermute | solution.py:16
  47.1 38.2 %copy-start.6 = (bf16[8,64,512]{2,1,0:T(8,128)(2,1)}, bf16[8,64,512]{2,1,0:T(8,128)(2,1)S(1)}, u32[]{:S(2)}) copy-start(bf16[8,64,512]{2,1,0:T(8,128)(2,1)S(1)} %collective-permute-done.5.refs_2_) | copy-start | bytes 1572868
  47.1 29.8 %collective-permute-start.19 = (bf16[8,64,512]{2,1,0:T(8,128)(2,1)S(1)}, bf16[8,64,512]{2,1,0:T(8,128)(2,1)S(1)}, u32[]{:S(2)}, u32[]{:S(2)}) collective-permute-start(bf16[8,64,512]{2,1,0:T(8,128)(2,1)S(1)} %collective-permute-done.7.refs_4_), channel_id=1, source_target_pairs={{2,6},{3,7},{4,0},{5,1},{10,14},{11,15},{12,8},{13,9},{18,22},{19,... | collective-permute-start | bytes 1572872 | tf_op jit(solution)/shard_map/ppermute | solution.py:16
  48.4 36.9 %copy-start.7 = (bf16[8,64,512]{2,1,0:T(8,128)(2,1)}, bf16[8,64,512]{2,1,0:T(8,128)(2,1)S(1)}, u32[]{:S(2)}) copy-start(bf16[8,64,512]{2,1,0:T(8,128)(2,1)S(1)} %collective-permute-done.4.refs_1_) | copy-start | bytes 1572868
  48.4 31.8 %collective-permute-start.8 = (bf16[8,64,512]{2,1,0:T(8,128)(2,1)S(1)}, bf16[8,64,512]{2,1,0:T(8,128)(2,1)}, u32[]{:S(2)}, u32[]{:S(2)}) collective-permute-start(bf16[8,64,512]{2,1,0:T(8,128)(2,1)S(1)} %collective-permute-done.7.refs_4_), channel_id=1, source_target_pairs={{1,0},{2,3},{5,4},{6,7},{9,8},{10,11},{13,12},{14,15},{17,16},{18,... | collective-permute-start | bytes 1572872 | tf_op jit(solution)/shard_map/ppermute | solution.py:16
  49.8 35.6 %copy-start.8 = (bf16[8,64,512]{2,1,0:T(8,128)(2,1)}, bf16[8,64,512]{2,1,0:T(8,128)(2,1)S(1)}, u32[]{:S(2)}) copy-start(bf16[8,64,512]{2,1,0:T(8,128)(2,1)S(1)} %collective-permute-done.13.refs_10_) | copy-start | bytes 1572868
  49.8 30.5 %collective-permute-start.21 = (bf16[8,64,512]{2,1,0:T(8,128)(2,1)S(1)}, bf16[8,64,512]{2,1,0:T(8,128)(2,1)}, u32[]{:S(2)}, u32[]{:S(2)}) collective-permute-start(bf16[8,64,512]{2,1,0:T(8,128)(2,1)S(1)} %collective-permute-done.5.refs_2_), channel_id=1, source_target_pairs={{0,6},{1,7},{6,0},{7,1},{8,14},{9,15},{14,8},{15,9},{16,22},{17,23... | collective-permute-start | bytes 1572872 | tf_op jit(solution)/shard_map/ppermute | solution.py:16
  54.2 26.6 %collective-permute-start.17 = (bf16[8,64,512]{2,1,0:T(8,128)(2,1)S(1)}, bf16[8,64,512]{2,1,0:T(8,128)(2,1)}, u32[]{:S(2)}, u32[]{:S(2)}) collective-permute-start(bf16[8,64,512]{2,1,0:T(8,128)(2,1)S(1)} %collective-permute-done.5.refs_2_), channel_id=1, source_target_pairs={{0,4},{1,5},{6,2},{7,3},{8,12},{9,13},{14,10},{15,11},{16,20},{17,... | collective-permute-start | bytes 1572872 | tf_op jit(solution)/shard_map/ppermute | solution.py:16
  68.5 13.6 %collective-permute-start.15 = (bf16[8,64,512]{2,1,0:T(8,128)(2,1)S(1)}, bf16[8,64,512]{2,1,0:T(8,128)(2,1)}, u32[]{:S(2)}, u32[]{:S(2)}) collective-permute-start(bf16[8,64,512]{2,1,0:T(8,128)(2,1)S(1)} %collective-permute-done.5.refs_2_), channel_id=1, source_target_pairs={{0,2},{1,3},{2,0},{3,1},{4,6},{5,7},{6,4},{7,5},{8,10},{9,11},{10,... | collective-permute-start | bytes 1572872 | tf_op jit(solution)/shard_map/ppermute | solution.py:16
  77.8 4.3 %collective-permute-start.6 = (bf16[8,64,512]{2,1,0:T(8,128)(2,1)S(1)}, bf16[8,64,512]{2,1,0:T(8,128)(2,1)}, u32[]{:S(2)}, u32[]{:S(2)}) collective-permute-start(bf16[8,64,512]{2,1,0:T(8,128)(2,1)S(1)} %collective-permute-done.5.refs_2_), channel_id=1, source_target_pairs={{0,1},{3,2},{4,5},{7,6},{8,9},{11,10},{12,13},{15,14},{16,17},{19,... | collective-permute-start | bytes 1572872 | tf_op jit(solution)/shard_map/ppermute | solution.py:16
  80.2 3.1 %collective-permute-start.14 = (bf16[8,64,512]{2,1,0:T(8,128)(2,1)S(1)}, bf16[8,64,512]{2,1,0:T(8,128)(2,1)}, u32[]{:S(2)}, u32[]{:S(2)}) collective-permute-start(bf16[8,64,512]{2,1,0:T(8,128)(2,1)S(1)} %collective-permute-done.13.refs_10_), channel_id=1, source_target_pairs={{0,1},{1,0},{2,3},{3,2},{4,5},{5,4},{6,7},{7,6},{8,9},{9,8},{10,11... | collective-permute-start | bytes 1572872 | tf_op jit(solution)/shard_map/ppermute | solution.py:16
  80.3 3.0 %collective-permute-start.20 = (bf16[8,64,512]{2,1,0:T(8,128)(2,1)}, bf16[8,64,512]{2,1,0:T(8,128)(2,1)}, u32[]{:S(2)}, u32[]{:S(2)}) collective-permute-start(bf16[8,64,512]{2,1,0:T(8,128)(2,1)} %copy-done.11), channel_id=1, source_target_pairs={{0,1},{1,0},{2,3},{3,2},{4,5},{5,4},{6,7},{7,6},{8,9},{9,8},{10,11... | collective-permute-start | bytes 1572872 | tf_op jit(solution)/shard_map/ppermute | solution.py:16
  80.8 3.0 %collective-permute-start.22 = (bf16[8,64,512]{2,1,0:T(8,128)(2,1)}, bf16[8,64,512]{2,1,0:T(8,128)(2,1)}, u32[]{:S(2)}, u32[]{:S(2)}) collective-permute-start(bf16[8,64,512]{2,1,0:T(8,128)(2,1)} %collective-permute-done.21.refs_18_), channel_id=1, source_target_pairs={{0,1},{1,0},{2,3},{3,2},{4,5},{5,4},{6,7},{7,6},{8,9},{9,8},{10,11... | collective-permute-start | bytes 1572872 | tf_op jit(solution)/shard_map/ppermute | solution.py:16
  82.1 2.5 %collective-permute-start.18 = (bf16[8,64,512]{2,1,0:T(8,128)(2,1)}, bf16[8,64,512]{2,1,0:T(8,128)(2,1)}, u32[]{:S(2)}, u32[]{:S(2)}) collective-permute-start(bf16[8,64,512]{2,1,0:T(8,128)(2,1)} %collective-permute-done.17.refs_14_), channel_id=1, source_target_pairs={{0,1},{1,0},{2,3},{3,2},{4,5},{5,4},{6,7},{7,6},{8,9},{9,8},{10,11... | collective-permute-start | bytes 1572872 | tf_op jit(solution)/shard_map/ppermute | solution.py:16
  82.1 3.2 %collective-permute-start.16 = (bf16[8,64,512]{2,1,0:T(8,128)(2,1)}, bf16[8,64,512]{2,1,0:T(8,128)(2,1)}, u32[]{:S(2)}, u32[]{:S(2)}) collective-permute-start(bf16[8,64,512]{2,1,0:T(8,128)(2,1)} %collective-permute-done.15.refs_12_), channel_id=1, source_target_pairs={{0,1},{1,0},{2,3},{3,2},{4,5},{5,4},{6,7},{7,6},{8,9},{9,8},{10,11... | collective-permute-start | bytes 1572872 | tf_op jit(solution)/shard_map/ppermute | solution.py:16
  98.6 14.5 %collective-permute-start.24 = (bf16[8,64,512]{2,1,0:T(8,128)(2,1)}, bf16[8,64,512]{2,1,0:T(8,128)(2,1)S(1)}, u32[]{:S(2)}, u32[]{:S(2)}) collective-permute-start(bf16[8,64,512]{2,1,0:T(8,128)(2,1)} %get-tuple-element.8.own_ref), channel_id=1, source_target_pairs={{0,2},{1,3},{2,0},{3,1},{4,6},{5,7},{6,4},{7,5},{8,10},{9,11},{10,... | collective-permute-start | bytes 1572872 | tf_op jit(solution)/shard_map/ppermute | solution.py:16
  99.9 13.3 %collective-permute-start.23 = (bf16[8,64,512]{2,1,0:T(8,128)(2,1)}, bf16[8,64,512]{2,1,0:T(8,128)(2,1)S(1)}, u32[]{:S(2)}, u32[]{:S(2)}) collective-permute-start(bf16[8,64,512]{2,1,0:T(8,128)(2,1)} %get-tuple-element.8.own_ref), channel_id=1, source_target_pairs={{0,1},{1,0},{2,3},{3,2},{4,5},{5,4},{6,7},{7,6},{8,9},{9,8},{10,11... | collective-permute-start | bytes 1572872 | tf_op jit(solution)/shard_map/ppermute | solution.py:16
  113.1 1.9 %collective-permute-start.25 = (bf16[8,64,512]{2,1,0:T(8,128)(2,1)S(1)}, bf16[8,64,512]{2,1,0:T(8,128)(2,1)S(1)}, u32[]{:S(2)}, u32[]{:S(2)}) collective-permute-start(bf16[8,64,512]{2,1,0:T(8,128)(2,1)S(1)} %collective-permute-done.24.x_ref), channel_id=1, source_target_pairs={{0,1},{1,0},{2,3},{3,2},{4,5},{5,4},{6,7},{7,6},{8,9},{9,8},{10,11... | collective-permute-start | bytes 1572872 | tf_op jit(solution)/shard_map/ppermute | solution.py:16
  (6 other events, 36.7 us)
